TPU v7x, 32 devices: a whole 2x2x4 slice. The times are simulated.
32 devices in a mesh: slab: 2 (over x), gal: 4 (over y, core), qb: 4 (over z).
Axes of the slice: x: 2, y: 2, z: 4, core: 2. Of those that a mesh axis runs over, the one named last changes fastest.
Arguments:
- gallery: bfloat16 [16384, 768], P(('slab', 'gal')), parts along dimension 0, may hold values from -512 to 512
- querybank: bfloat16 [8, 2048, 768], P(('slab', 'qb'), 'gal'), parts along dimension 0, may hold values from -512 to 512
- test_queries: bfloat16 [8, 512, 768], P(('slab', 'qb'), 'gal'), parts along dimension 0, may hold values from -512 to 512
Outputs:
- logprob: float32 [4096, 8192], P(('slab', 'qb'), 'gal'), parts along dimension 0
- normalizer: float32 [16384], P(('slab', 'gal')), parts along dimension 0
There are 2 independent parts, one for each index of `slab`. A program takes and returns all parts, laid end to end along the dimension named above; each array names one. Nothing has to cross between parts.
All inputs are finite; a program needn't handle non-finite values.
Results may differ from a plain program's by a relative error of at most 0.00049.
Values may be sent and summed in bfloat16 or wider, within the bound.
No kernel may reach another device: no remote copies, remote signals or barrier semaphores. Data moves between devices by JAX's collectives and lax.ppermute only.
A program may use at most 64 MiB of HBM per device.

v0:
```python
import math
import jax
import jax.numpy as jnp
from jax import lax
from jax.sharding import PartitionSpec as P

sharpness = 20.0


def unit_rows(values):
    wide = values.astype(jnp.float32)
    scaled = wide * lax.rsqrt(jnp.sum(wide * wide, axis=-1, keepdims=True) + 1e-06)
    return scaled.astype(jnp.bfloat16)


def column_terms(bank_block, gallery_unit):
    scores = lax.dot_general(
        bank_block, gallery_unit, (((1,), (1,)), ((), ())), preferred_element_type=jnp.float32
    )
    return jnp.sum(jnp.exp(sharpness * (scores - 1.0)), axis=0)


def bank_columns(bank_block, gallery_unit):
    rows = bank_block.shape[0]
    height = math.gcd(rows, 512)

    def add_block(index, running):
        piece = lax.dynamic_slice_in_dim(bank_block, index * height, height, 0)
        return running + column_terms(piece, gallery_unit)

    initial = jnp.zeros((gallery_unit.shape[0],), jnp.float32)
    return lax.fori_loop(0, rows // height, add_block, initial)


def per_device(gallery, querybank, test_queries):
    gallery_unit = unit_rows(gallery)
    bank_local = unit_rows(querybank[0])
    test_local = unit_rows(test_queries[0])
    bank_all = lax.all_gather(bank_local, "gal", axis=0, tiled=True)
    column_part = bank_columns(bank_all, gallery_unit)
    test_all = lax.all_gather(test_local, "gal", axis=0, tiled=True)
    column_total = lax.psum(column_part, "qb")
    normalizer = sharpness + jnp.log(column_total)
    bank_count = querybank.shape[1] * lax.axis_size("gal") * lax.axis_size("qb")
    offset = 2.0 * sharpness - math.log(bank_count)
    scores = lax.dot_general(
        test_all, gallery_unit, (((1,), (1,)), ((), ())), preferred_element_type=jnp.float32
    )
    logits = sharpness * scores - normalizer[None, :] - offset
    row_part = jnp.sum(jnp.exp(logits), axis=1)
    row_total = lax.psum(row_part, "gal")
    logprob = logits - jnp.log(row_total)[:, None]
    return (logprob, normalizer)


def solution(mesh):
    placed = (
        P(("slab", "gal"), None),
        P(("slab", "qb"), "gal", None),
        P(("slab", "qb"), "gal", None),
    )
    return jax.shard_map(
        per_device,
        mesh=mesh,
        in_specs=placed,
        out_specs=(P(("slab", "qb"), "gal"), P(("slab", "gal"))),
        check_vma=False,
    )
```

profile of v0, /device:TPU:0, one launch (start us, length us, event | category | flops | bytes accessed | tf_op | source)
XLA Modules:
  0.0 94.0 jit_solution(4073056862240279345)
XLA Ops:
  7.2 0.0 copy-start.1
  7.2 0.0 copy-start
  7.2 0.0 all-gather.2.cloned.1.call-start
  7.2 1.5 %fusion.5 = f32[512]{0:T(512)S(1)} fusion(bf16[1,512,768]{2,1,0:T(8,128)(2,1)} %param.6), kind=kLoop, calls=%fused_computation.13 | loop fusion | flops 1179136 | bytes 788480 | tf_op jit(solution)/shard_map/reduce_sum | solution.py:12
  8.8 2.2 %fusion.6 = bf16[512,768]{1,0:T(8,128)(2,1)} fusion(bf16[1,512,768]{2,1,0:T(8,128)(2,1)} %param.6, f32[512]{0:T(512)S(1)} %add_rsqrt_fusion.1), kind=kLoop, calls=%fused_computation.14 | loop fusion | flops 1179648 | bytes 1574912 | tf_op jit(solution)/shard_map/convert_element_type | solution.py:13
  11.0 0.0 all-gather.2.cloned.1.call-update
  11.0 1.0 %fusion.7 = f32[128]{0:T(128)S(1)} fusion(bf16[1,128,768]{2,1,0:T(8,128)(2,1)} %param.7), kind=kLoop, calls=%fused_computation.17 | loop fusion | flops 294784 | bytes 197120 | tf_op jit(solution)/shard_map/reduce_sum | solution.py:12
  12.1 0.0 copy-done
  12.1 0.7 fusion.2
  12.8 0.0 copy-done.1
  12.8 0.1 fusion.8
  12.9 10.6 %all_gather.6 = bf16[512,768]{1,0:T(8,128)(2,1)} all-gather(bf16[128,768]{1,0:T(8,128)(2,1)S(1)} %fusion.8), channel_id=1, replica_groups=mesh['slab'=2,'gal'=4,'qb'=4] {'gal'}, dimensions={0}, use_global_device_ids=true | all-gather | bytes 983040 | tf_op jit(solution)/shard_map/all_gather | solution.py:41
  23.5 2.3 %fusion.3 = bf16[2048,768]{1,0:T(8,128)(2,1)} fusion(bf16[2048,768]{1,0:T(8,128)(2,1)S(1)} %copy-done, f32[2048]{0:T(1024)S(1)} %add_rsqrt_fusion), kind=kLoop, calls=%fused_computation.7 | loop fusion | flops 4718592 | bytes 6299648 | tf_op jit(solution)/shard_map/convert_element_type | solution.py:13
  25.8 16.6 %all-gather.2.cloned.1.call-done = bf16[2048,768]{1,0:T(8,128)(2,1)} async-done(((bf16[512,768]{1,0:T(8,128)(2,1)}), bf16[2048,768]{1,0:T(8,128)(2,1)}) %all-gather.2.cloned.1.call-update) | async-done | bytes 3145744 | tf_op jit(solution)/shard_map/all_gather | solution.py:39
  42.4 16.3 %while.16 = (s32[]{:T(128)}, f32[2048]{0:T(1024)S(1)}, bf16[2048,768]{1,0:T(8,128)(2,1)}, bf16[2048,768]{1,0:T(8,128)(2,1)}, s32[]{:T(128)}, /*index=5*/s32[]{:T(128)}, s32[]{:T(128)}, s32[]{:T(128)}) while((s32[]{:T(128)}, f32[2048]{0:T(1024)S(1)}, bf16[2048,768]{1,0:T(8,128)(2,1)}, bf16[2048,768]{1,0:T(8,128)(2,1)}, s32[]{:T(128)}, ...), condition=%wide.region_5.0_spmd.clone, body=%wide.region_3.0_spmd.clone.sunk | while | flops 1613760512 | bytes 3965081 | solution.py:32
  42.4 4.1 %exponential_reduce_fusion.3 = f32[2048]{0:T(1024)S(1)} fusion(bf16[2048,768]{1,0:T(8,128)(2,1)} %get-tuple-element.182, bf16[2048,768]{1,0:T(8,128)(2,1)} %get-tuple-element.181, s32[]{:T(128)S(6)} %select_n.12), kind=kOutput, calls=%fused_computation.clone.1 | convolution fusion | flops 1613756416 | bytes 3940356 | tf_op jit(solution)/shard_map/while/body/eval_jaxpr/dot_general | solution.py:17
  46.5 4.0 %exponential_reduce_fusion.3 = f32[2048]{0:T(1024)S(1)} fusion(bf16[2048,768]{1,0:T(8,128)(2,1)} %get-tuple-element.182, bf16[2048,768]{1,0:T(8,128)(2,1)} %get-tuple-element.181, s32[]{:T(128)S(6)} %select_n.12), kind=kOutput, calls=%fused_computation.clone.1 | convolution fusion | flops 1613756416 | bytes 3940356 | tf_op jit(solution)/shard_map/while/body/eval_jaxpr/dot_general | solution.py:17
  50.6 4.0 %exponential_reduce_fusion.3 = f32[2048]{0:T(1024)S(1)} fusion(bf16[2048,768]{1,0:T(8,128)(2,1)} %get-tuple-element.182, bf16[2048,768]{1,0:T(8,128)(2,1)} %get-tuple-element.181, s32[]{:T(128)S(6)} %select_n.12), kind=kOutput, calls=%fused_computation.clone.1 | convolution fusion | flops 1613756416 | bytes 3940356 | tf_op jit(solution)/shard_map/while/body/eval_jaxpr/dot_general | solution.py:17
  54.6 4.0 %exponential_reduce_fusion.3 = f32[2048]{0:T(1024)S(1)} fusion(bf16[2048,768]{1,0:T(8,128)(2,1)} %get-tuple-element.182, bf16[2048,768]{1,0:T(8,128)(2,1)} %get-tuple-element.181, s32[]{:T(128)S(6)} %select_n.12), kind=kOutput, calls=%fused_computation.clone.1 | convolution fusion | flops 1613756416 | bytes 3940356 | tf_op jit(solution)/shard_map/while/body/eval_jaxpr/dot_general | solution.py:17
  58.7 11.8 %psum.14 = f32[2048]{0:T(1024)S(1)} all-reduce(f32[2048]{0:T(1024)S(1)} %get-tuple-element.112), channel_id=1, replica_groups=mesh['slab'=2,'gal'=4,'qb'=4] {'qb'}, use_global_device_ids=true, to_apply=%region_6.0 | all-reduce | flops 2048 | bytes 16384 | tf_op jit(solution)/shard_map/psum | solution.py:42
  70.5 0.0 copy-start.3
  70.6 5.9 %exponential_reduce_fusion.1 = (f32[512]{0:T(512)S(1)}, f32[512,2048]{1,0:T(8,128)}) fusion(f32[2048]{0:T(1024)S(1)} %log_add_fusion, bf16[512,768]{1,0:T(8,128)(2,1)S(1)} %copy-done.2, bf16[2048,768]{1,0:T(8,128)(2,1)} %get-tuple-element.188), kind=kOutput, calls=%fused_computation.8 | convolution fusion | flops 1614806528 | bytes 8136704 | tf_op jit(solution)/shard_map/dot_general | solution.py:46
  76.5 5.9 %psum.15 = f32[512]{0:T(512)S(1)} all-reduce(f32[512]{0:T(512)S(1)} %get-tuple-element.136), channel_id=1, replica_groups=mesh['slab'=2,'gal'=4,'qb'=4] {'gal'}, use_global_device_ids=true, to_apply=%region_8.0 | all-reduce | flops 512 | bytes 4096 | tf_op jit(solution)/shard_map/psum | solution.py:51
  82.4 4.8 %fusion.4 = f32[512,2048]{1,0:T(8,128)} fusion(f32[512,2048]{1,0:T(8,128)} %get-tuple-element.137, f32[512]{0:T(512)S(1)} %log.7, f32[2048]{0:T(1024)S(1)} %log_add_fusion), kind=kLoop, calls=%fused_computation.10 | loop fusion | flops 4194304 | bytes 8398848 | tf_op jit(solution)/shard_map/sub | solution.py:52
  (13 shorter events, 0.1 us)
Async XLA Ops:
  7.2 5.6 %copy-start.1 = (bf16[1,128,768]{2,1,0:T(8,128)(2,1)S(1)}, bf16[1,128,768]{2,1,0:T(8,128)(2,1)}, u32[]{:S(2)}) copy-start(bf16[1,128,768]{2,1,0:T(8,128)(2,1)} %param.7) | copy-start | bytes 589828
  7.2 4.9 %copy-start = (bf16[2048,768]{1,0:T(8,128)(2,1)S(1)}, bf16[2048,768]{1,0:T(8,128)(2,1)}, u32[]{:S(2)}) copy-start(bf16[2048,768]{1,0:T(8,128)(2,1)} %param.5) | copy-start | bytes 9437188
  7.2 35.2 %all-gather.2.cloned.1.call-start = ((), (), s32[]{:S(2)}) async-start(), calls=%async_computation | async-start | bytes 3932160 | tf_op jit(solution)/shard_map/all_gather | solution.py:39
  42.4 28.2 %copy-start.2 = (bf16[512,768]{1,0:T(8,128)(2,1)S(1)}, bf16[512,768]{1,0:T(8,128)(2,1)}, u32[]{:S(2)}) copy-start(bf16[512,768]{1,0:T(8,128)(2,1)} %all_gather.6) | copy-start | bytes 2359300
  70.5 11.9 %copy-start.3 = (f32[2048]{0:T(1024)}, f32[2048]{0:T(1024)S(1)}, u32[]{:S(2)}) copy-start(f32[2048]{0:T(1024)S(1)} %log_add_fusion) | copy-start | bytes 24580
Sparse Core Ops, SparseCore 0:
  11.1 31.2 all-gather.1
where the time goes:
time: 94.4 us; the launch traced here: 94 us
  blocking collectives  28.3 us (30%)
  matrix products  22.1 us (23%)
  waiting for transfers between devices  16.6 us (18%)
  between operations  14.1 us (15%)
  other arithmetic  12.7 us (13%)
    all_gather x1, waiting for transfers between devices, per_device(): bank_all = lax.all_gather(bank_local, 'gal', axis=0, tiled=True)  16.6 us
    dot_general x4, matrix products, column_terms(): lax.dot_general(bank_block, gallery_unit, (((1,), (1,)), ((), ())), prefe...  16.1 us
    psum x1, blocking collectives, per_device(): column_total = lax.psum(column_part, 'qb')  11.8 us
    all_gather x1, blocking collectives, per_device(): test_all = lax.all_gather(test_local, 'gal', axis=0, tiled=True)  10.6 us
    dot_general x1, matrix products, per_device(): lax.dot_general(test_all, gallery_unit, (((1,), (1,)), ((), ())), preferr...  5.95 us
    psum x1, blocking collectives, per_device(): row_total = lax.psum(row_part, 'gal')  5.9 us
    sub x1, other arithmetic, per_device(): logprob = logits - jnp.log(row_total)[:, None]  4.79 us
    convert_element_type x3, other arithmetic, unit_rows(): return scaled.astype(jnp.bfloat16)  4.59 us
  transfers between devices with their start and end apart: 1, of which 1 were waited for; matrix products, arithmetic and copies ran while one was open for 4% of the time, Pallas kernels for 0%

commit v1 on v0

--- a/solution.py
+++ b/solution.py
@@ -38,7 +38,12 @@
     test_local = unit_rows(test_queries[0])
     bank_all = lax.all_gather(bank_local, "gal", axis=0, tiled=True)
     column_part = bank_columns(bank_all, gallery_unit)
-    test_all = lax.all_gather(test_local, "gal", axis=0, tiled=True)
+    ring = [test_local]
+    for hop in range(3):
+        ring.append(lax.ppermute(ring[-1], "gal", [(dev, (dev + 1) % 4) for dev in range(4)]))
+    test_all = jnp.roll(
+        jnp.concatenate(ring[::-1], axis=0), (lax.axis_index("gal") + 1) * ring[0].shape[0], axis=0
+    )
     column_total = lax.psum(column_part, "qb")
     normalizer = sharpness + jnp.log(column_total)
     bank_count = querybank.shape[1] * lax.axis_size("gal") * lax.axis_size("qb")

time: 94.4 us -> 91.5 us (0.969)
  blocking collectives: 28.3 us -> 17.5 us
  local copies, waits for them, and re-layouts: 0.03 us -> 7.84 us
  matrix products: 22.1 us -> 17.2 us
  waiting for transfers between devices: 16.6 us -> 20.4 us
    ppermute x0 -> x3, waiting for transfers between devices: none -> 17.2 us  [per_device(): lax.ppermute(ring[-1], 'gal', [(dev, (dev + 1) % 4) for dev in range(4)])]
    all_gather x1, waiting for transfers between devices: 16.6 us -> 3.19 us  [per_device(): bank_all = lax.all_gather(bank_local, 'gal', axis=0, tiled=True)]
    all_gather x1 -> x0, blocking collectives: 10.6 us -> none  [per_device(): test_all = lax.all_gather(test_local, 'gal', axis=0, tiled=True)]
    unnamed x8 -> x14, local copies, waits for them, and re-layouts: 0.02 us -> 7.83 us
    dot_general x4, matrix products: 16.1 us -> 12 us  [column_terms(): lax.dot_general(bank_block, gallery_unit, (((1,), (1,)), ((), ())), prefe...]
  transfers between devices with their start and end apart: 1 -> 4, of which waited for: 1 -> 4; matrix products, arithmetic and copies ran while one was open for 4% -> 14% of each run, Pallas kernels for 0% -> 0%
where the time goes in v1:
time: 91.5 us; the launch traced here: 91 us
  waiting for transfers between devices  20.4 us (22%)
  blocking collectives  17.5 us (19%)
  matrix products  17.2 us (19%)
  between operations  14.1 us (15%)
  other arithmetic  13.3 us (15%)
  local copies, waits for them, and re-layouts  7.84 us (9%)
    ppermute x3, waiting for transfers between devices, per_device(): lax.ppermute(ring[-1], 'gal', [(dev, (dev + 1) % 4) for dev in range(4)])  17.2 us
    dot_general x4, matrix products, column_terms(): lax.dot_general(bank_block, gallery_unit, (((1,), (1,)), ((), ())), prefe...  12 us
    psum x1, blocking collectives, per_device(): column_total = lax.psum(column_part, 'qb')  11.9 us
    unnamed x14, local copies, waits for them, and re-layouts  7.83 us
    psum x1, blocking collectives, per_device(): row_total = lax.psum(row_part, 'gal')  5.63 us
    dot_general x1, matrix products, per_device(): lax.dot_general(test_all, gallery_unit, (((1,), (1,)), ((), ())), preferr...  5.17 us
    sub x1, other arithmetic, per_device(): logprob = logits - jnp.log(row_total)[:, None]  4.79 us
    convert_element_type x3, other arithmetic, unit_rows(): return scaled.astype(jnp.bfloat16)  4.57 us
  transfers between devices with their start and end apart: 4, of which 4 were waited for; matrix products, arithmetic and copies ran while one was open for 14% of the time, Pallas kernels for 0%

profile of v1, /device:TPU:0, one launch (start us, length us, event | category | flops | bytes accessed | tf_op | source)
XLA Modules:
  0.0 91.0 jit_solution(16841833736631148777)
XLA Ops:
  7.2 1.5 %fusion.5 = f32[512]{0:T(512)S(1)} fusion(bf16[1,512,768]{2,1,0:T(8,128)(2,1)} %param.6), kind=kLoop, calls=%fused_computation.13 | loop fusion | flops 1179136 | bytes 788480 | tf_op jit(solution)/shard_map/reduce_sum | solution.py:12
  8.8 2.2 %fusion.6 = bf16[512,768]{1,0:T(8,128)(2,1)} fusion(bf16[1,512,768]{2,1,0:T(8,128)(2,1)} %param.6, f32[512]{0:T(512)S(1)} %add_rsqrt_fusion.1), kind=kLoop, calls=%fused_computation.14 | loop fusion | flops 1179648 | bytes 1574912 | tf_op jit(solution)/shard_map/convert_element_type | solution.py:13
  11.8 0.7 fusion.2
  12.5 4.6 %collective-permute-done = bf16[128,768]{1,0:T(8,128)(2,1)S(1)} collective-permute-done((bf16[128,768]{1,0:T(8,128)(2,1)S(1)}, bf16[128,768]{1,0:T(8,128)(2,1)S(1)}, u32[]{:S(2)}, u32[]{:S(2)}) %collective-permute-start) | collective-permute-done | bytes 196640 | tf_op jit(solution)/shard_map/ppermute | solution.py:43
  17.1 5.2 %collective-permute-done.1 = bf16[128,768]{1,0:T(8,128)(2,1)} collective-permute-done((bf16[128,768]{1,0:T(8,128)(2,1)S(1)}, bf16[128,768]{1,0:T(8,128)(2,1)}, u32[]{:S(2)}, u32[]{:S(2)}) %collective-permute-start.1) | collective-permute-done | bytes 196640 | tf_op jit(solution)/shard_map/ppermute | solution.py:43
  22.3 2.2 %fusion.3 = bf16[2048,768]{1,0:T(8,128)(2,1)} fusion(bf16[2048,768]{1,0:T(8,128)(2,1)S(1)} %copy-done, f32[2048]{0:T(1024)S(1)} %add_rsqrt_fusion), kind=kLoop, calls=%fused_computation.7 | loop fusion | flops 4718592 | bytes 6299648 | tf_op jit(solution)/shard_map/convert_element_type | solution.py:13
  24.5 7.4 %collective-permute-done.2 = bf16[128,768]{1,0:T(8,128)(2,1)} collective-permute-done((bf16[128,768]{1,0:T(8,128)(2,1)}, bf16[128,768]{1,0:T(8,128)(2,1)}, u32[]{:S(2)}, u32[]{:S(2)}) %collective-permute-start.2) | collective-permute-done | bytes 196640 | tf_op jit(solution)/shard_map/ppermute | solution.py:43
  31.9 1.6 %constant_dynamic-update-slice_fusion.7 = bf16[1024,768]{1,0:T(8,128)(2,1)} fusion(bf16[128,768]{1,0:T(8,128)(2,1)} %collective-permute-done.2), kind=kLoop, calls=%fused_computation.28 | loop fusion | bytes 393216
  33.6 1.6 %constant_dynamic-update-slice_fusion.6 = bf16[1024,768]{1,0:T(8,128)(2,1)} fusion(bf16[1024,768]{1,0:T(8,128)(2,1)} %constant_dynamic-update-slice_fusion.7, bf16[128,768]{1,0:T(8,128)(2,1)} %collective-permute-done.1), kind=kLoop, calls=%fused_computation.27 | loop fusion | bytes 393216
  35.9 0.8 constant_dynamic-update-slice_fusion.4
  36.6 1.6 %constant_dynamic-update-slice_fusion.3 = bf16[1024,768]{1,0:T(8,128)(2,1)} fusion(bf16[1024,768]{1,0:T(8,128)(2,1)} %constant_dynamic-update-slice_fusion.4, bf16[128,768]{1,0:T(8,128)(2,1)} %collective-permute-done.2), kind=kLoop, calls=%fused_computation.24 | loop fusion | bytes 393216
  38.2 1.6 %constant_dynamic-update-slice_fusion.2 = bf16[1024,768]{1,0:T(8,128)(2,1)} fusion(bf16[1024,768]{1,0:T(8,128)(2,1)} %constant_dynamic-update-slice_fusion.3, bf16[128,768]{1,0:T(8,128)(2,1)} %collective-permute-done.1), kind=kLoop, calls=%fused_computation.23 | loop fusion | bytes 393216
  39.8 0.7 constant_dynamic-update-slice_fusion.1
  40.5 0.8 constant_dynamic-update-slice_fusion
  41.3 3.2 %all-gather.2.cloned.1.call-done = bf16[2048,768]{1,0:T(8,128)(2,1)} async-done(((bf16[512,768]{1,0:T(8,128)(2,1)}), bf16[2048,768]{1,0:T(8,128)(2,1)}) %all-gather.2.cloned.1.call-update) | async-done | bytes 3145744 | tf_op jit(solution)/shard_map/all_gather | solution.py:39
  44.5 12.2 %while.16 = (s32[]{:T(128)}, f32[2048]{0:T(1024)S(1)}, bf16[2048,768]{1,0:T(8,128)(2,1)}, bf16[2048,768]{1,0:T(8,128)(2,1)S(1)}, s32[]{:T(128)}, /*index=5*/s32[]{:T(128)}, s32[]{:T(128)}, s32[]{:T(128)}) while((s32[]{:T(128)}, f32[2048]{0:T(1024)S(1)}, bf16[2048,768]{1,0:T(8,128)(2,1)}, bf16[2048,768]{1,0:T(8,128)(2,1)S(1)}, ...), condition=%wide.region_5.0_spmd.clone, body=%wide.region_3.0_spmd.clone.sunk | while | flops 1613760512 | bytes 3965081 | solution.py:32
  44.5 3.0 %exponential_reduce_fusion.3 = f32[2048]{0:T(1024)S(1)} fusion(bf16[2048,768]{1,0:T(8,128)(2,1)S(1)} %get-tuple-element.182, bf16[2048,768]{1,0:T(8,128)(2,1)} %get-tuple-element.181, s32[]{:T(128)S(6)} %select_n.27), kind=kOutput, calls=%fused_computation.clone.1 | convolution fusion | flops 1613756416 | bytes 3940356 | tf_op jit(solution)/shard_map/while/body/eval_jaxpr/dot_general | solution.py:17
  47.6 3.0 %exponential_reduce_fusion.3 = f32[2048]{0:T(1024)S(1)} fusion(bf16[2048,768]{1,0:T(8,128)(2,1)S(1)} %get-tuple-element.182, bf16[2048,768]{1,0:T(8,128)(2,1)} %get-tuple-element.181, s32[]{:T(128)S(6)} %select_n.27), kind=kOutput, calls=%fused_computation.clone.1 | convolution fusion | flops 1613756416 | bytes 3940356 | tf_op jit(solution)/shard_map/while/body/eval_jaxpr/dot_general | solution.py:17
  50.6 3.0 %exponential_reduce_fusion.3 = f32[2048]{0:T(1024)S(1)} fusion(bf16[2048,768]{1,0:T(8,128)(2,1)S(1)} %get-tuple-element.182, bf16[2048,768]{1,0:T(8,128)(2,1)} %get-tuple-element.181, s32[]{:T(128)S(6)} %select_n.27), kind=kOutput, calls=%fused_computation.clone.1 | convolution fusion | flops 1613756416 | bytes 3940356 | tf_op jit(solution)/shard_map/while/body/eval_jaxpr/dot_general | solution.py:17
  53.7 3.0 %exponential_reduce_fusion.3 = f32[2048]{0:T(1024)S(1)} fusion(bf16[2048,768]{1,0:T(8,128)(2,1)S(1)} %get-tuple-element.182, bf16[2048,768]{1,0:T(8,128)(2,1)} %get-tuple-element.181, s32[]{:T(128)S(6)} %select_n.27), kind=kOutput, calls=%fused_computation.clone.1 | convolution fusion | flops 1613756416 | bytes 3940356 | tf_op jit(solution)/shard_map/while/body/eval_jaxpr/dot_general | solution.py:17
  56.7 11.9 %psum.14 = f32[2048]{0:T(1024)S(1)} all-reduce(f32[2048]{0:T(1024)S(1)} %get-tuple-element.112), channel_id=1, replica_groups=mesh['slab'=2,'gal'=4,'qb'=4] {'qb'}, use_global_device_ids=true, to_apply=%region_6.7 | all-reduce | flops 2048 | bytes 16384 | tf_op jit(solution)/shard_map/psum | solution.py:47
  68.6 5.2 %exponential_reduce_fusion.1 = (f32[512]{0:T(512)S(1)}, f32[512,2048]{1,0:T(8,128)}) fusion(f32[2048]{0:T(1024)S(1)} %log_add_fusion, bf16[2048,768]{1,0:T(8,128)(2,1)S(1)} %get-tuple-element.188, bf16[1024,768]{1,0:T(8,128)(2,1)} %constant_dynamic-update-slice_fusion, s32[]{:T(128)S(6)} %select_n.24), kind=kOutput, calls=%fused_computation.8 | convolution fusion | flops 1614806528 | bytes 8136708 | tf_op jit(solution)/shard_map/dot_general | solution.py:51
  73.8 5.6 %psum.15 = f32[512]{0:T(512)S(1)} all-reduce(f32[512]{0:T(512)S(1)} %get-tuple-element.136), channel_id=1, replica_groups=mesh['slab'=2,'gal'=4,'qb'=4] {'gal'}, use_global_device_ids=true, to_apply=%region_8.9 | all-reduce | flops 512 | bytes 4096 | tf_op jit(solution)/shard_map/psum | solution.py:56
  79.4 4.8 %fusion.4 = f32[512,2048]{1,0:T(8,128)} fusion(f32[512,2048]{1,0:T(8,128)} %get-tuple-element.137, f32[512]{0:T(512)S(1)} %log.7, f32[2048]{0:T(1024)S(1)} %log_add_fusion), kind=kLoop, calls=%fused_computation.10 | loop fusion | flops 4194304 | bytes 8398848 | tf_op jit(solution)/shard_map/sub | solution.py:57
  (26 shorter events, 1.6 us)
Async XLA Ops:
  7.2 3.8 %copy-start.2 = (bf16[1,128,768]{2,1,0:T(8,128)(2,1)S(1)}, bf16[1,128,768]{2,1,0:T(8,128)(2,1)}, u32[]{:S(2)}) copy-start(bf16[1,128,768]{2,1,0:T(8,128)(2,1)} %param.7) | copy-start | bytes 589828
  7.2 4.6 %copy-start = (bf16[2048,768]{1,0:T(8,128)(2,1)S(1)}, bf16[2048,768]{1,0:T(8,128)(2,1)}, u32[]{:S(2)}) copy-start(bf16[2048,768]{1,0:T(8,128)(2,1)} %param.5) | copy-start | bytes 9437188
  7.2 37.3 %all-gather.2.cloned.1.call-start = ((), (), s32[]{:S(2)}) async-start(), calls=%async_computation | async-start | bytes 3932160 | tf_op jit(solution)/shard_map/all_gather | solution.py:39
  11.3 5.8 %collective-permute-start = (bf16[128,768]{1,0:T(8,128)(2,1)S(1)}, bf16[128,768]{1,0:T(8,128)(2,1)S(1)}, u32[]{:S(2)}, u32[]{:S(2)}) collective-permute-start(bf16[128,768]{1,0:T(8,128)(2,1)S(1)} %fusion.10), channel_id=1, source_target_pairs={{0,4},{4,8},{8,12},{12,0},{1,5},{5,9},{9,13},{13,1},{2,6},{6,10},{... | collective-permute-start | bytes 589832 | tf_op jit(solution)/shard_map/ppermute | solution.py:43
  17.1 5.2 %collective-permute-start.1 = (bf16[128,768]{1,0:T(8,128)(2,1)S(1)}, bf16[128,768]{1,0:T(8,128)(2,1)}, u32[]{:S(2)}, u32[]{:S(2)}) collective-permute-start(bf16[128,768]{1,0:T(8,128)(2,1)S(1)} %collective-permute-done), channel_id=1, source_target_pairs={{0,4},{4,8},{8,12},{12,0},{1,5},{5,9},{9,13},{13,1},{2,6},{6,10},{... | collective-permute-start | bytes 589832 | tf_op jit(solution)/shard_map/ppermute | solution.py:43
  22.3 9.6 %collective-permute-start.2 = (bf16[128,768]{1,0:T(8,128)(2,1)}, bf16[128,768]{1,0:T(8,128)(2,1)}, u32[]{:S(2)}, u32[]{:S(2)}) collective-permute-start(bf16[128,768]{1,0:T(8,128)(2,1)} %collective-permute-done.1), channel_id=1, source_target_pairs={{0,4},{4,8},{8,12},{12,0},{1,5},{5,9},{9,13},{13,1},{2,6},{6,10},{... | collective-permute-start | bytes 589832 | tf_op jit(solution)/shard_map/ppermute | solution.py:43
  24.5 20.0 %copy-start.1 = (bf16[2048,768]{1,0:T(8,128)(2,1)S(1)}, bf16[2048,768]{1,0:T(8,128)(2,1)}, u32[]{:S(2)}) copy-start(bf16[2048,768]{1,0:T(8,128)(2,1)} %fusion.3) | copy-start | bytes 9437188
  68.6 10.8 %copy-start.3 = (f32[2048]{0:T(1024)}, f32[2048]{0:T(1024)S(1)}, u32[]{:S(2)}) copy-start(f32[2048]{0:T(1024)S(1)} %log_add_fusion) | copy-start | bytes 24580
Sparse Core Ops, SparseCore 0:
  11.1 33.3 all-gather.1
